TPU v7x, 256 devices: a whole 4x4x8 slice. The times are simulated.
256 devices in a mesh: lev: 4 (over z_hi, core), tile: 64 (over z_lo, x, y).
Axes of the slice: x: 4, y: 4, z: 8 (z_hi: 2, z_lo: 4; z = z_hi * 4 + z_lo), core: 2. Of those that a mesh axis runs over, the one named last changes fastest.
Arguments:
- adjoint_final: float32 [6, 96, 512, 128], P(None, 'lev', 'tile'), may hold values from -6 to 6
- courant_x: float32 [96, 512, 128], P('lev', 'tile'), may hold values from 0.05 to 0.45
- courant_y: float32 [96, 512, 128], P('lev', 'tile'), may hold values from 0.05 to 0.45
- sound: float32 [96], P('lev'), may hold values from 0.1 to 0.5
- phys_jac: bfloat16 [4, 576, 576], replicated, as said below
- regime: int32 [4, 512, 128], P(None, 'tile'), may hold values from 0 to 3
- obs_operator: bfloat16 [128, 6, 96], P(None, None, 'lev'), may hold values from -0.5 to 0.5
- obs_rows: bfloat16 [4, 131072, 128], P(None, 'tile'), may hold values from -6 to 6
- obs_owner: int32 [4, 131072, 1], P(None, 'tile'), may hold values from 0 to 63; in each aligned block of 2048 rows (0 to 2047, 2048 to 4095, ..., all dimensions but the last counted through in order) at most 64 rows name the same one
- obs_cell: int32 [4, 131072], P(None, 'tile'), may hold values from 0 to 1023
- obs_count: int32 [4, 64], P(None, 'tile'), may hold values from 1 to 2048, 98304 in all within a row
Outputs:
- gradient: float32 [6, 96, 512, 128], P(None, 'lev', 'tile')
Inputs may be any that keep to these rules, and one draw needn't show every extreme that they name: `obs_owner`: among the rows of one device in one step, at most 64 name one owner. `phys_jac`: A square matrix per regime.
All inputs are finite; a program needn't handle non-finite values. No bound on the sum of `obs_count` on one device may be relied on, other than what follows from the above.
Results may differ from a plain program's by a relative error of at most 0.0015.
Values may be sent and summed in bfloat16 or wider, within the bound.
A program may use at most 128 MiB of HBM per device.

v0:
```python
import jax
import jax.numpy as jnp
import numpy as np
from jax import lax
from jax.experimental import pallas as pl
from jax.experimental.pallas import tpu as pltpu
from jax.sharding import PartitionSpec as P

MESH = pl.DeviceIdType.MESH
BF = jnp.bfloat16
F32 = jnp.float32
NT = (((1,), (1,)), ((), ()))
GROUP = 8


def iota(shape, dim):
    return lax.broadcasted_iota(jnp.int32, shape, dim)


def owner_lev(t, d, lev, per_z):
    h = lev // 2
    c = lev % 2
    apart = jnp.abs(t // per_z - d // per_z)
    return jnp.where(apart == 3, 1 - h, h) * 2 + c


def kernel(
    lam_ref, cx_ref, cy_ref, sound_ref, reg_ref, op_ref, own_ref, cell_ref, cnt_ref,
    jac_hbm, perm_hbm, rows_hbm, out_ref,
    rows_v, send_rows, recv_rows, send_cell, recv_cell, oh, rc, rank_s, own_s, pmat, key_s, ohs, acc, g_s,
    a_s, b_s, lam_out, misc, misc_out, op_s, jac_s, perm_s, jt_s, col,
    e_in, w_in, e_out, w_out, cxe_in, cxe_out, fin_in,
    load_sem, ss_rows, rs_rows, ss_cell, rs_cell, gs_sem, gr_sem,
    xs_sem, xr_sem, es, er, ws, wr, cs, cr, ks, kr, ts, tr,
):
    lev = lax.axis_index("lev")
    t = lax.axis_index("tile")
    _, n_tile, cap, vals = send_rows.shape
    obs = rows_v.shape[1]
    per_z = n_tile // 4
    h = lev // 2
    c = lev % 2
    core = lev + 1 - 2 * c
    far = (lev + 2) % 4
    steps, half_x, width_all, ny = col.shape
    nx = 2 * half_x
    width = a_s.shape[2]
    nl = misc.shape[2]
    nf = width // nl
    low = h == t % 2
    x0 = jnp.where(low, 0, half_x)
    x1 = half_x - x0
    groups = n_tile // GROUP
    my_group = t // GROUP
    own_rows = pl.ds(pl.multiple_of(c * 2 * width, 16), 2 * width)

    w_lev, w_tile = jnp.where(low, lev, far), jnp.where(low, t - 1, t)
    e_lev, e_tile = jnp.where(low, far, lev), jnp.where(low, t, t + 1)
    has_west = w_tile >= 0
    has_east = e_tile < n_tile

    def remote(src, dst, ssem, rsem, to_lev, to_tile):
        return pltpu.make_async_remote_copy(
            src_ref=src, dst_ref=dst, send_sem=ssem, recv_sem=rsem,
            device_id={"lev": to_lev, "tile": to_tile}, device_id_type=MESH,
        )

    load_rows = [
        pltpu.make_async_copy(rows_hbm.at[c + 2 * j], rows_v.at[j], load_sem.at[j]) for j in range(2)
    ]
    load_jac = pltpu.make_async_copy(jac_hbm, jac_s, load_sem.at[2])
    load_perm = pltpu.make_async_copy(perm_hbm, perm_s, load_sem.at[3])
    for load in load_rows + [load_jac, load_perm]:
        load.start()

    barrier = pltpu.get_barrier_semaphore()

    def greet(i, _):
        d = (t + i) % n_tile
        pl.semaphore_signal(
            barrier, inc=1, device_id={"lev": owner_lev(t, d, lev, per_z), "tile": d}, device_id_type=MESH
        )
        return 0

    lax.fori_loop(1, n_tile, greet, 0)
    for other in (core, far):
        pl.semaphore_signal(barrier, inc=1, device_id={"lev": other, "tile": t}, device_id_type=MESH)

    def columns(ref, x, rows):
        return ref[pl.ds(x, rows, stride=nx), :]

    same = iota((nl, nl), 0) == iota((nl, nl), 1)
    hs = 0.5 * jnp.sum(jnp.where(same, sound_ref[...], 0.0), axis=1, keepdims=True)
    hs = jnp.broadcast_to(hs, (nl, ny))
    for i in range(half_x):
        lam_out[i] = columns(lam_ref, x1 + i, width)
        misc_out[i] = columns(cx_ref, x1 + i, nl)
        misc_out[half_x + i] = columns(cy_ref, x1 + i, nl)
        a_s[i, h] = columns(lam_ref, x0 + i, width)
        misc[h, i] = columns(cx_ref, x0 + i, nl)
        misc[h, half_x + i] = columns(cy_ref, x0 + i, nl)
    for ref in (misc_out, misc.at[h]):
        ref[nx] = hs
        ref[nx + 1] = columns(cx_ref, half_x, nl)
    op_s[h] = op_ref[...]

    cx_goes = jnp.logical_and(low, has_west)
    cx_comes = jnp.logical_and(jnp.logical_not(low), has_east)

    @pl.when(jnp.logical_not(cx_comes))
    def _():
        cxe_in[...] = jnp.zeros_like(cxe_in)

    @pl.when(jnp.logical_not(has_west))
    def _():
        w_in[...] = jnp.zeros_like(w_in)

    @pl.when(jnp.logical_not(has_east))
    def _():
        e_in[...] = jnp.zeros_like(e_in)

    pl.semaphore_wait(barrier, n_tile + 1)

    order = [0, half_x - 1] + list(range(1, half_x - 1))
    swap_misc = remote(misc_out, misc.at[h], xs_sem.at[half_x], xr_sem.at[half_x], far, t)
    swap_op = remote(op_s.at[h], op_s.at[h], xs_sem.at[half_x + 1], xr_sem.at[half_x + 1], far, t)
    swap_lam = [remote(lam_out.at[i], a_s.at[i, h], xs_sem.at[i], xr_sem.at[i], far, t) for i in range(half_x)]
    swap_misc.start()
    for i in order:
        swap_lam[i].start()
    swap_op.start()

    upper = jnp.where(iota((128, 256), 0) < iota((128, 256), 1), 1.0, 0.0).astype(BF)
    lane128 = iota((n_tile, 128), 1)

    def rank_rows(j):
        step = c + 2 * j
        live = iota((1, obs), 1) < cnt_ref[0, step]
        own = jnp.where(live, own_ref[step], -1)
        own_s[j] = own
        oh[...] = jnp.where(own == iota((n_tile, obs), 0), 1.0, 0.0).astype(BF)
        carry = jnp.zeros((n_tile, 128), F32)
        for b in range(obs // 128):
            cols = slice(b * 128, (b + 1) * 128)
            hot = oh[:, cols]
            ex = jnp.dot(hot, upper, preferred_element_type=F32)
            rank_s[j, :, cols] = jnp.sum(hot.astype(F32) * (ex[:, :128] + carry), axis=0, keepdims=True)
            carry = carry + ex[:, 128:]
        rank = jnp.where(live, rank_s[j], -1.0)
        rank_s[j] = rank
        cell = cell_ref[pl.ds(step, 1), :]
        hot = rank == iota((cap, obs), 0).astype(F32)
        rc[:cap] = jnp.where(hot, (cell >> 7).astype(F32), 0.0).astype(BF)
        rc[cap:] = jnp.where(hot, ((cell & 127) + 1).astype(F32), 0.0).astype(BF)
        both = lax.dot_general(oh[...], rc[...], NT, preferred_element_type=F32)
        key = both * 128.0 + pltpu.roll(both, 64, axis=1)
        return jnp.where(lane128 < 64, key, 0.0)

    def cell_copy(d):
        return remote(
            send_cell.at[pl.ds(d, 1), :], recv_cell.at[pl.ds(t, 1), :], ss_cell.at[d], rs_cell.at[t],
            owner_lev(t, d, lev, per_z), d,
        )

    def row_copy(j, d):
        return remote(
            send_rows.at[j, d], recv_rows.at[j, t], ss_rows.at[j, d], rs_rows.at[j, t],
            owner_lev(t, d, lev, per_z), d,
        )

    def arrival(buf, sem, s):
        return remote(buf, buf, sem, sem, owner_lev(t, s, lev, per_z), s)

    sub16 = iota((16, obs), 0).astype(F32)

    def pack_rows(j):
        load_rows[j].wait()

        def pack(g, _):
            d0 = pl.multiple_of(((g + my_group) % groups) * GROUP, GROUP)
            for i in range(GROUP):
                key = jnp.where(own_s[j] == d0 + i, rank_s[j], -1.0)
                key = jnp.broadcast_to(key, (16, obs)).astype(BF)
                for q in range(cap // 16):
                    hot = key == (sub16 + 16.0 * q).astype(BF)
                    pmat[i * cap + q * 16 : i * cap + (q + 1) * 16, :] = jnp.where(
                        hot, jnp.ones((), BF), jnp.zeros((), BF)
                    )
            packed = jnp.dot(pmat[...], rows_v[j], preferred_element_type=F32)
            send_rows[j, pl.ds(d0, GROUP)] = packed.astype(BF).reshape(GROUP, cap, vals)

            def send(i, _):
                d = d0 + i

                @pl.when(d != t)
                def _():
                    row_copy(j, d).start()

                return 0

            lax.fori_loop(0, GROUP, send, 0)
            return 0

        lax.fori_loop(0, groups, pack, 0)
        recv_rows[j, t] = send_rows[j, t]

    key0 = rank_rows(0)
    pack_rows(0)
    send_cell[...] = key0 + pltpu.roll(rank_rows(1), 64, axis=1)

    def send_cells(i, _):
        cell_copy((t + i) % n_tile).start()
        return 0

    lax.fori_loop(1, n_tile, send_cells, 0)
    recv_cell[pl.ds(t, 1), :] = send_cell[pl.ds(t, 1), :]

    def to_west(n):
        return remote(e_out.at[n], e_in.at[n], es.at[n], er.at[n], w_lev, w_tile)

    def to_east(n):
        return remote(w_out.at[n], w_in.at[n], ws.at[n], wr.at[n], e_lev, e_tile)

    cx_west = remote(cxe_out, cxe_in, cs, cr, w_lev, w_tile)

    def send_halos(n, src):
        for b in range(2):
            e_out[n, b] = src[0, b].astype(BF)
            last = src[half_x - 1, b]
            w_out[n, b] = jnp.concatenate([last[:nl], last[3 * nl : 4 * nl]], axis=0).astype(BF)

        @pl.when(has_west)
        def _():
            to_west(n).start()

        @pl.when(has_east)
        def _():
            to_east(n).start()

    def wait_halos(n):
        @pl.when(has_east)
        def _():
            to_west(n).wait_recv()

        @pl.when(has_west)
        def _():
            to_east(n).wait_recv()

    swap_misc.wait_recv()
    for i in (0, half_x - 1):
        swap_lam[i].wait_recv()
    for b in range(2):
        cxe_out[b] = misc[b, 0]
    @pl.when(cx_goes)
    def _():
        cx_west.start()

    send_halos(0, a_s)

    load_jac.wait()
    load_perm.wait()
    regimes = jac_s.shape[0]
    for r in range(regimes):
        mine = lax.dot_general(perm_s[own_rows, :], jac_s[r], NT, preferred_element_type=F32).astype(BF)
        mine = lax.dot_general(mine, perm_s[...], NT, preferred_element_type=F32).astype(BF)
        jt_s[r * 2 * width : (r + 1) * 2 * width, :] = mine

    pack_rows(1)

    lane = iota((width, ny), 1)
    lane1 = iota((nl, ny), 1)

    def north(v):
        inside = (lane if v.shape[0] == width else lane1) < ny - 1
        return jnp.where(inside, pltpu.roll(v, ny - 1, axis=1), 0.0)

    def south(v):
        inside = (lane if v.shape[0] == width else lane1) > 0
        return jnp.where(inside, pltpu.roll(v, 1, axis=1), 0.0)

    def field(v, f):
        return v[f * nl : (f + 1) * nl]

    def to_core(n, x):
        part = col.at[n, x, own_rows, :]
        return remote(part, part, ks.at[n, x], kr.at[n, x], core, t)

    def dyn(n, x, src, dst):
        for b in range(2):
            me = src[x, b]
            cx, cy, hl = misc[b, x], misc[b, half_x + x], misc[b, nx]
            if x == half_x - 1:
                east = e_in[n, b].astype(F32)
                cxe = jnp.where(low, misc[b, nx + 1], cxe_in[b])
            else:
                east, cxe = src[x + 1, b], misc[b, x + 1]
            if x == 0:
                west = w_in[n, b].astype(F32)
                west_u, west_p = west[:nl], west[nl:]
            else:
                west_u, west_p = src[x - 1, b, :nl], src[x - 1, b, 3 * nl : 4 * nl]
            tile = lambda v: jnp.concatenate([v] * nf, axis=0)
            new = me + tile(cxe) * east + north(tile(cy) * me) - tile(cx + cy) * me
            v, p = field(me, 1), field(me, 3)
            d_u = hl * (field(east, 3) - west_p)
            d_v = hl * (north(p) - south(p))
            d_p = hl * (field(east, 0) - west_u + north(v) - south(v))
            zero = jnp.zeros_like(d_u)
            new = new + jnp.concatenate([d_u, d_v, zero, d_p, zero, zero], axis=0)
            dst[x, b] = new
            col[n, x, pl.ds(pl.multiple_of(c * 2 * width + b * width, 16), width), :] = new.astype(BF)
        to_core(n, x).start()

    def phys(n, xs, dst):
        for x in xs:
            to_core(n, x).wait_recv()
        both = jnp.concatenate([col[n, x] for x in xs], axis=1)
        out = jnp.dot(jt_s[...], both, preferred_element_type=F32)
        ops = [jnp.concatenate([op_s[b], op_s[b]], axis=1) for b in range(2)]
        for at, x in enumerate(xs):
            part = out[:, at * ny : (at + 1) * ny]
            reg = reg_ref[pl.ds(n * nx + x0 + x, 1), :]
            sums = g_s[n, x * ny : (x + 1) * ny, :]
            for b in range(2):
                delta = part[b * width : (b + 1) * width]
                for r in range(1, regimes):
                    row = (2 * r + b) * width
                    delta = jnp.where(reg == r, part[row : row + width], delta)
                forcing = lax.dot_general(ops[b], sums, NT, preferred_element_type=F32)
                dst[x, b] = dst[x, b] + delta.astype(BF).astype(F32) + forcing

    def cells_in(i, _):
        s = (t + n_tile - i) % n_tile
        arrival(recv_cell.at[pl.ds(s, 1), :], rs_cell.at[s], s).wait_recv()
        return 0

    def read_cells():
        lax.fori_loop(1, n_tile, cells_in, 0)
        even = recv_cell[pl.ds(0, n_tile // 2, stride=2), :]
        odd = recv_cell[pl.ds(1, n_tile // 2, stride=2), :]
        left = iota((n_tile // 2, 128), 1) < 64
        key_s[0] = jnp.where(left, even, pltpu.roll(odd, 64, axis=1)).astype(jnp.int32) - 1
        key_s[1] = jnp.where(left, pltpu.roll(even, 64, axis=1), odd).astype(jnp.int32) - 1

    sub16s = iota((16, GROUP * cap), 0).astype(F32)

    def sum_rows(j, first, last):
        def unpack(g, _):
            s0 = pl.multiple_of(((groups - g + my_group) % groups) * GROUP, GROUP)

            def take(i, _):
                s = s0 + i

                @pl.when(s != t)
                def _():
                    arrival(recv_rows.at[j, s], rs_rows.at[j, s], s).wait_recv()

                return 0

            lax.fori_loop(0, GROUP, take, 0)
            key = jnp.concatenate(
                [key_s[j, pl.ds(s0 // 2 + q, 1), :] for q in range(GROUP // 2)], axis=1
            )
            at_x = (key >> 7) - x0
            at_y = (key & 127).astype(F32)
            for x in range(half_x):
                kx = jnp.broadcast_to(jnp.where(at_x == x, at_y, -1.0), (16, GROUP * cap)).astype(BF)
                for q in range(ny // 16):
                    hot = kx == (sub16s + 16.0 * q).astype(BF)
                    ohs[x * ny + q * 16 : x * ny + (q + 1) * 16, :] = jnp.where(
                        hot, jnp.ones((), BF), jnp.zeros((), BF)
                    )
            rows = recv_rows[j, pl.ds(s0, GROUP)].reshape(GROUP * cap, vals)
            acc[...] += jnp.dot(ohs[...], rows, preferred_element_type=F32)
            return 0

        if first == 0:
            acc[...] = jnp.zeros_like(acc)
        lax.fori_loop(first, last, unpack, 0)

    def share(j):
        part = g_s.at[c + 2 * j]
        return remote(part, part, gs_sem.at[j], gr_sem.at[j], core, t)

    def share_sums(j):
        total = acc[...]
        head = total.astype(BF)
        g_s[c + 2 * j, :, :vals] = head
        g_s[c + 2 * j, :, vals:] = (total - head.astype(F32)).astype(BF)
        share(j).start()

    for i in range(1, half_x - 1):
        swap_lam[i].wait_recv()

    @pl.when(cx_comes)
    def _():
        cx_west.wait_recv()

    inner = list(range(1, half_x - 1))
    outer = [0, half_x - 1]
    for x in inner:
        dyn(0, x, a_s, b_s)
    wait_halos(0)
    for x in outer:
        dyn(0, x, a_s, b_s)
    read_cells()
    sum_rows(0, 0, groups)
    share_sums(0)
    swap_op.wait_recv()
    now, new = b_s, a_s
    for n in range(steps):
        if n == 0:
            share(0).wait_recv()
        if n == 2:
            share(1).wait_recv()
        phys(n, outer, now)
        if n + 1 < steps:
            send_halos(n + 1, now)
        else:
            finish(outer, now, fin_in, ts, tr, h, far, t, remote)
        phys(n, inner, now)
        if n + 1 == steps:
            finish(inner, now, fin_in, ts, tr, h, far, t, remote)
            break
        if n == 0:
            sum_rows(1, 0, groups // 2)
        if n == 1:
            sum_rows(1, groups // 2, groups)
            share_sums(1)
        for x in inner:
            dyn(n + 1, x, now, new)
        wait_halos(n + 1)
        for x in outer:
            dyn(n + 1, x, now, new)
        now, new = new, now

    for i in range(half_x):
        out_ref[pl.ds(x0 + i, width, stride=nx), :] = now[i, h]
    for i in outer + inner:
        remote(now.at[i, 1 - h], fin_in.at[i], ts.at[i], tr.at[i], far, t).wait_recv()
        out_ref[pl.ds(x1 + i, width, stride=nx), :] = fin_in[i]

    def drain(i, _):
        d = (t + i) % n_tile
        cell_copy(d).wait_send()
        for j in range(2):
            row_copy(j, d).wait_send()
        return 0

    lax.fori_loop(1, n_tile, drain, 0)
    for copy in [swap_misc, swap_op] + swap_lam + [share(0), share(1)]:
        copy.wait_send()

    @pl.when(cx_goes)
    def _():
        cx_west.wait_send()

    for i in range(half_x):
        remote(now.at[i, 1 - h], fin_in.at[i], ts.at[i], tr.at[i], far, t).wait_send()
    for n in range(steps):
        for x in range(half_x):
            to_core(n, x).wait_send()

        @pl.when(has_west)
        def _(n=n):
            to_west(n).wait_send()

        @pl.when(has_east)
        def _(n=n):
            to_east(n).wait_send()


def finish(xs, now, fin_in, ts, tr, h, far, t, remote):
    for x in xs:
        remote(now.at[x, 1 - h], fin_in.at[x], ts.at[x], tr.at[x], far, t).start()


def place_of(levels_all, lev_here, fields):
    core, far, f, l = np.meshgrid(
        np.arange(2), np.arange(2), np.arange(fields), np.arange(lev_here), indexing="ij"
    )
    place = (f * levels_all + (2 * far + core) * lev_here + l).reshape(-1)
    return (place[:, None] == np.arange(place.size)[None, :]).astype(np.float32)


def on_device(
    adjoint_final,
    courant_x,
    courant_y,
    sound,
    phys_jac,
    regime,
    obs_operator,
    obs_rows,
    obs_owner,
    obs_cell,
    obs_count,
):
    fields, nl, nx, ny = adjoint_final.shape
    n_tile = lax.axis_size("tile")
    n_lev = lax.axis_size("lev")
    steps, obs, vals = obs_rows.shape
    cap = max(2, 2 * obs // n_tile)
    regimes = phys_jac.shape[0]
    width = fields * nl
    width_all = width * n_lev
    hx = nx // 2
    perm = jnp.asarray(place_of(nl * n_lev, nl, fields), BF)
    vmem = pl.BlockSpec(memory_space=pltpu.VMEM)
    hbm = pl.BlockSpec(memory_space=pl.ANY)
    V = pltpu.VMEM
    dma = pltpu.SemaphoreType.DMA
    out = pl.pallas_call(
        kernel,
        out_shape=jax.ShapeDtypeStruct((width * nx, ny), F32),
        in_specs=[vmem] * 8 + [pl.BlockSpec(memory_space=pltpu.SMEM)] + [hbm] * 3,
        out_specs=vmem,
        scratch_shapes=[
            V((2, obs, vals), BF),
            V((2, n_tile, cap, vals), BF),
            V((2, n_tile, cap, vals), BF),
            V((n_tile, 128), F32),
            V((n_tile, 128), F32),
            V((n_tile, obs), BF),
            V((2 * cap, obs), BF),
            V((2, 1, obs), F32),
            V((2, 1, obs), jnp.int32),
            V((GROUP * cap, obs), BF),
            V((2, n_tile // 2, 128), jnp.int32),
            V((hx * ny, GROUP * cap), BF),
            V((hx * ny, vals), F32),
            V((steps, hx * ny, 2 * vals), BF),
            V((hx, 2, width, ny), F32),
            V((hx, 2, width, ny), F32),
            V((hx, width, ny), F32),
            V((2, nx + 2, nl, ny), F32),
            V((nx + 2, nl, ny), F32),
            V((2, width, vals), BF),
            V((regimes, width_all, width_all), BF),
            V((width_all, width_all), BF),
            V((regimes * 2 * width, width_all), BF),
            V((steps, hx, width_all, ny), BF),
            V((steps, 2, width, ny), BF),
            V((steps, 2, 2 * nl, ny), BF),
            V((steps, 2, width, ny), BF),
            V((steps, 2, 2 * nl, ny), BF),
            V((2, nl, ny), F32),
            V((2, nl, ny), F32),
            V((hx, width, ny), F32),
            dma((4,)), dma((2, n_tile)), dma((2, n_tile)), dma((n_tile,)), dma((n_tile,)), dma((2,)), dma((2,)),
            dma((hx + 2,)), dma((hx + 2,)), dma((steps,)), dma((steps,)), dma((steps,)), dma((steps,)),
            dma, dma, dma((steps, hx)), dma((steps, hx)), dma((hx,)), dma((hx,)),
        ],
        compiler_params=pltpu.CompilerParams(
            collective_id=0, has_side_effects=True, vmem_limit_bytes=56 * 1024 * 1024
        ),
        name="sweep",
    )(
        adjoint_final.reshape(width * nx, ny),
        courant_x.reshape(nl * nx, ny),
        courant_y.reshape(nl * nx, ny),
        sound.reshape(1, nl),
        regime.reshape(steps * nx, ny),
        obs_operator.transpose(1, 2, 0).reshape(width, vals),
        obs_owner.reshape(steps, 1, obs),
        obs_cell,
        obs_count.reshape(1, steps),
        phys_jac,
        perm,
        obs_rows,
    )
    return out.reshape(adjoint_final.shape)


def solution(mesh):
    return jax.shard_map(
        on_device,
        mesh=mesh,
        in_specs=(
            P(None, "lev", "tile", None),
            P("lev", "tile", None),
            P("lev", "tile", None),
            P("lev"),
            P(),
            P(None, "tile", None),
            P(None, None, "lev"),
            P(None, "tile", None),
            P(None, "tile", None),
            P(None, "tile"),
            P(None, "tile"),
        ),
        out_specs=P(None, "lev", "tile", None),
        check_vma=False,
    )
```

profile of v0, /device:TPU:63, one launch (start us, length us, event | category | flops | bytes accessed | tf_op | source)
XLA Modules:
  0.0 119.2 jit_solution(6188988490258054156)
XLA Ops:
  0.0 117.3 %sweep.1 = f32[1152,128]{1,0:T(8,128)} custom-call(f32[1152,128]{1,0:T(8,128)} %bitcast.12, f32[192,128]{1,0:T(8,128)} %bitcast.13, f32[192,128]{1,0:T(8,128)} %bitcast.14, f32[1,24]{1,0:T(1,128)} %bitcast.18, s32[32,128]{1,0:T(8,128)} %bitcast.17, bf16[144,128]{1,0:T(8,128)(2,1)} %bitcast.15, s32[4,1,2048]{2,1,0:T(1,128)} %bitcast.16, s32[4,2048]{1,0:T(4,128)} %cell_ref.1, ...), custom_call_target="tpu_custom_call" | custom-call | tf_op jit(solution)/shard_map/sweep/pallas_call | solution.py:513
  117.3 1.9 %copy.14 = f32[6,24,8,128]{3,2,1,0:T(8,128)} copy(f32[6,24,8,128]{3,2,1,0:T(8,128)} %bitcast.11) | data formatting | bytes 1179648
where the time goes:
time: 119 us
  Pallas kernels  117 us (98%)
  local copies, waits for them, and re-layouts  1.92 us (2%)
    pallas_call x1, Pallas kernels, on_device(): pl.pallas_call(kernel, out_shape=jax.ShapeDtypeStruct((width * nx, ny), F...  117 us

commit v1 on v0

--- a/solution.py
+++ b/solution.py
@@ -17,27 +17,27 @@
     return lax.broadcasted_iota(jnp.int32, shape, dim)
 
 
-def owner_lev(t, d, lev, per_z):
-    h = lev // 2
-    c = lev % 2
+def crosses(t, d, n_tile):
+    per_z = n_tile // 4
     apart = jnp.abs(t // per_z - d // per_z)
-    return jnp.where(apart == 3, 1 - h, h) * 2 + c
+    odd = (t // GROUP + d // GROUP) % 2 == 1
+    return jnp.logical_or(apart == 3, jnp.logical_and(apart == 2, odd))
 
 
 def kernel(
-    lam_ref, cx_ref, cy_ref, sound_ref, reg_ref, op_ref, own_ref, cell_ref, cnt_ref,
-    jac_hbm, perm_hbm, rows_hbm, out_ref,
-    rows_v, send_rows, recv_rows, send_cell, recv_cell, oh, rc, rank_s, own_s, pmat, key_s, ohs, acc, g_s,
+    sound_ref, reg_ref, op_ref, own_ref, cell_ref, cnt_ref,
+    lam_hbm, cx_hbm, cy_hbm, jac_hbm, perm_hbm, rows_hbm, out_hbm,
+    lam_ref, cx_ref, cy_ref,
+    rows_v, send_rows, recv_rows, send_cell, recv_cell, oh, rc, rank_s, own_s, pmat, key_s, ohs, acc, g_s, g_far,
     a_s, b_s, lam_out, misc, misc_out, op_s, jac_s, perm_s, jt_s, col,
-    e_in, w_in, e_out, w_out, cxe_in, cxe_out, fin_in,
-    load_sem, ss_rows, rs_rows, ss_cell, rs_cell, gs_sem, gr_sem,
-    xs_sem, xr_sem, es, er, ws, wr, cs, cr, ks, kr, ts, tr,
+    e_in, w_in, e_out, w_out, cxe_in, cxe_out,
+    load_sem, ss_rows, rs_rows, ss_cell, rs_cell, gks, gkr, gzs, gzr, gfs, gfr,
+    xs_sem, xr_sem, es, er, ws, wr, cs, cr, ks, kr, ts, tr, ls,
 ):
     lev = lax.axis_index("lev")
     t = lax.axis_index("tile")
-    _, n_tile, cap, vals = send_rows.shape
+    n_tile, cap, vals = send_rows.shape
     obs = rows_v.shape[1]
-    per_z = n_tile // 4
     h = lev // 2
     c = lev % 2
     core = lev + 1 - 2 * c
@@ -65,12 +65,16 @@
             device_id={"lev": to_lev, "tile": to_tile}, device_id_type=MESH,
         )
 
-    load_rows = [
-        pltpu.make_async_copy(rows_hbm.at[c + 2 * j], rows_v.at[j], load_sem.at[j]) for j in range(2)
+    mine = lev
+    sent_steps = (lev, far)
+    load_rows = [pltpu.make_async_copy(rows_hbm.at[n], rows_v.at[j], load_sem.at[j]) for j, n in enumerate(sent_steps)]
+    load_jac = pltpu.make_async_copy(jac_hbm, jac_s, load_sem.at[2])
+    load_perm = pltpu.make_async_copy(perm_hbm, perm_s, load_sem.at[6])
+    load_state = [
+        pltpu.make_async_copy(src, dst, load_sem.at[3 + i])
+        for i, (src, dst) in enumerate(((lam_hbm, lam_ref), (cx_hbm, cx_ref), (cy_hbm, cy_ref)))
     ]
-    load_jac = pltpu.make_async_copy(jac_hbm, jac_s, load_sem.at[2])
-    load_perm = pltpu.make_async_copy(perm_hbm, perm_s, load_sem.at[3])
-    for load in load_rows + [load_jac, load_perm]:
+    for load in load_state + load_rows + [load_jac, load_perm]:
         load.start()
 
     barrier = pltpu.get_barrier_semaphore()
@@ -78,7 +82,7 @@
     def greet(i, _):
         d = (t + i) % n_tile
         pl.semaphore_signal(
-            barrier, inc=1, device_id={"lev": owner_lev(t, d, lev, per_z), "tile": d}, device_id_type=MESH
+            barrier, inc=1, device_id={"lev": jnp.where(crosses(t, d, n_tile), far, lev), "tile": d}, device_id_type=MESH
         )
         return 0
 
@@ -92,6 +96,8 @@
     same = iota((nl, nl), 0) == iota((nl, nl), 1)
     hs = 0.5 * jnp.sum(jnp.where(same, sound_ref[...], 0.0), axis=1, keepdims=True)
     hs = jnp.broadcast_to(hs, (nl, ny))
+    for load in load_state:
+        load.wait()
     for i in range(half_x):
         lam_out[i] = columns(lam_ref, x1 + i, width)
         misc_out[i] = columns(cx_ref, x1 + i, nl)
@@ -121,7 +127,10 @@
 
     pl.semaphore_wait(barrier, n_tile + 1)
 
-    order = [0, half_x - 1] + list(range(1, half_x - 1))
+    inner = list(range(1, half_x - 1))
+    outer = [0, half_x - 1]
+    order = outer + inner
+    slot = {x: i for i, x in enumerate(order)}
     swap_misc = remote(misc_out, misc.at[h], xs_sem.at[half_x], xr_sem.at[half_x], far, t)
     swap_op = remote(op_s.at[h], op_s.at[h], xs_sem.at[half_x + 1], xr_sem.at[half_x + 1], far, t)
     swap_lam = [remote(lam_out.at[i], a_s.at[i, h], xs_sem.at[i], xr_sem.at[i], far, t) for i in range(half_x)]
@@ -134,7 +143,7 @@
     lane128 = iota((n_tile, 128), 1)
 
     def rank_rows(j):
-        step = c + 2 * j
+        step = sent_steps[j]
         live = iota((1, obs), 1) < cnt_ref[0, step]
         own = jnp.where(live, own_ref[step], -1)
         own_s[j] = own
@@ -158,26 +167,28 @@
 
     def cell_copy(d):
         return remote(
-            send_cell.at[pl.ds(d, 1), :], recv_cell.at[pl.ds(t, 1), :], ss_cell.at[d], rs_cell.at[t],
-            owner_lev(t, d, lev, per_z), d,
+            send_cell.at[crosses(t, d, n_tile).astype(jnp.int32), pl.ds(d, 1), :], recv_cell.at[pl.ds(t, 1), :],
+            ss_cell, rs_cell, jnp.where(crosses(t, d, n_tile), far, lev), d,
         )
 
-    def row_copy(j, d):
+    def row_copy(d):
         return remote(
-            send_rows.at[j, d], recv_rows.at[j, t], ss_rows.at[j, d], rs_rows.at[j, t],
-            owner_lev(t, d, lev, per_z), d,
+            send_rows.at[d], recv_rows.at[t], ss_rows, rs_rows.at[my_group],
+            jnp.where(crosses(t, d, n_tile), far, lev), d,
         )
 
-    def arrival(buf, sem, s):
-        return remote(buf, buf, sem, sem, owner_lev(t, s, lev, per_z), s)
+    def all_of(buf, ssem, rsem):
+        return remote(buf, buf, ssem, rsem, far, t)
 
     sub16 = iota((16, obs), 0).astype(F32)
 
-    def pack_rows(j):
-        load_rows[j].wait()
+    def pack_rows():
+        for load in load_rows:
+            load.wait()
 
         def pack(g, _):
             d0 = pl.multiple_of(((g + my_group) % groups) * GROUP, GROUP)
+            j = crosses(t, d0, n_tile).astype(jnp.int32)
             for i in range(GROUP):
                 key = jnp.where(own_s[j] == d0 + i, rank_s[j], -1.0)
                 key = jnp.broadcast_to(key, (16, obs)).astype(BF)
@@ -187,14 +198,14 @@
                         hot, jnp.ones((), BF), jnp.zeros((), BF)
                     )
             packed = jnp.dot(pmat[...], rows_v[j], preferred_element_type=F32)
-            send_rows[j, pl.ds(d0, GROUP)] = packed.astype(BF).reshape(GROUP, cap, vals)
+            send_rows[pl.ds(d0, GROUP)] = packed.astype(BF).reshape(GROUP, cap, vals)
 
             def send(i, _):
                 d = d0 + i
 
                 @pl.when(d != t)
                 def _():
-                    row_copy(j, d).start()
+                    row_copy(d).start()
 
                 return 0
 
@@ -202,18 +213,19 @@
             return 0
 
         lax.fori_loop(0, groups, pack, 0)
-        recv_rows[j, t] = send_rows[j, t]
-
-    key0 = rank_rows(0)
-    pack_rows(0)
-    send_cell[...] = key0 + pltpu.roll(rank_rows(1), 64, axis=1)
+        recv_rows[t] = send_rows[t]
+
+    for j in range(2):
+        keys = rank_rows(j)
+        send_cell[j] = jnp.where(t % 2 == 0, keys, pltpu.roll(keys, 64, axis=1))
 
     def send_cells(i, _):
         cell_copy((t + i) % n_tile).start()
         return 0
 
     lax.fori_loop(1, n_tile, send_cells, 0)
-    recv_cell[pl.ds(t, 1), :] = send_cell[pl.ds(t, 1), :]
+    recv_cell[pl.ds(t, 1), :] = send_cell[0, pl.ds(t, 1), :]
+    pack_rows()
 
     def to_west(n):
         return remote(e_out.at[n], e_in.at[n], es.at[n], er.at[n], w_lev, w_tile)
@@ -245,6 +257,14 @@
         @pl.when(has_west)
         def _():
             to_east(n).wait_recv()
+
+    load_jac.wait()
+    load_perm.wait()
+    regimes = jac_s.shape[0]
+    for r in range(regimes):
+        part = lax.dot_general(perm_s[own_rows, :], jac_s[r], NT, preferred_element_type=F32).astype(BF)
+        part = lax.dot_general(part, perm_s[...], NT, preferred_element_type=F32).astype(BF)
+        jt_s[r * 2 * width : (r + 1) * 2 * width, :] = part
 
     swap_misc.wait_recv()
     for i in (0, half_x - 1):
@@ -256,16 +276,6 @@
         cx_west.start()
 
     send_halos(0, a_s)
-
-    load_jac.wait()
-    load_perm.wait()
-    regimes = jac_s.shape[0]
-    for r in range(regimes):
-        mine = lax.dot_general(perm_s[own_rows, :], jac_s[r], NT, preferred_element_type=F32).astype(BF)
-        mine = lax.dot_general(mine, perm_s[...], NT, preferred_element_type=F32).astype(BF)
-        jt_s[r * 2 * width : (r + 1) * 2 * width, :] = mine
-
-    pack_rows(1)
 
     lane = iota((width, ny), 1)
     lane1 = iota((nl, ny), 1)
@@ -320,7 +330,7 @@
         for at, x in enumerate(xs):
             part = out[:, at * ny : (at + 1) * ny]
             reg = reg_ref[pl.ds(n * nx + x0 + x, 1), :]
-            sums = g_s[n, x * ny : (x + 1) * ny, :]
+            sums = g_s[n, slot[x]]
             for b in range(2):
                 delta = part[b * width : (b + 1) * width]
                 for r in range(1, regimes):
@@ -329,48 +339,41 @@
                 forcing = lax.dot_general(ops[b], sums, NT, preferred_element_type=F32)
                 dst[x, b] = dst[x, b] + delta.astype(BF).astype(F32) + forcing
 
-    def cells_in(i, _):
-        s = (t + n_tile - i) % n_tile
-        arrival(recv_cell.at[pl.ds(s, 1), :], rs_cell.at[s], s).wait_recv()
-        return 0
-
     def read_cells():
-        lax.fori_loop(1, n_tile, cells_in, 0)
+        all_of(recv_cell.at[pl.ds(0, n_tile - 1), :], ss_cell, rs_cell).wait_recv()
         even = recv_cell[pl.ds(0, n_tile // 2, stride=2), :]
         odd = recv_cell[pl.ds(1, n_tile // 2, stride=2), :]
-        left = iota((n_tile // 2, 128), 1) < 64
-        key_s[0] = jnp.where(left, even, pltpu.roll(odd, 64, axis=1)).astype(jnp.int32) - 1
-        key_s[1] = jnp.where(left, pltpu.roll(even, 64, axis=1), odd).astype(jnp.int32) - 1
+        key_s[...] = (even + odd).astype(jnp.int32) - 1
 
     sub16s = iota((16, GROUP * cap), 0).astype(F32)
 
-    def sum_rows(j, first, last):
+    def sum_rows(first, last):
         def unpack(g, _):
             s0 = pl.multiple_of(((groups - g + my_group) % groups) * GROUP, GROUP)
 
-            def take(i, _):
-                s = s0 + i
-
-                @pl.when(s != t)
-                def _():
-                    arrival(recv_rows.at[j, s], rs_rows.at[j, s], s).wait_recv()
-
-                return 0
-
-            lax.fori_loop(0, GROUP, take, 0)
+            from_group = s0 // GROUP
+
+            @pl.when(from_group != my_group)
+            def _():
+                all_of(recv_rows.at[pl.ds(0, GROUP)], ss_rows, rs_rows.at[from_group]).wait_recv()
+
+            @pl.when(from_group == my_group)
+            def _():
+                all_of(recv_rows.at[pl.ds(0, GROUP - 1)], ss_rows, rs_rows.at[from_group]).wait_recv()
+
             key = jnp.concatenate(
-                [key_s[j, pl.ds(s0 // 2 + q, 1), :] for q in range(GROUP // 2)], axis=1
+                [key_s[pl.ds(s0 // 2 + q, 1), :] for q in range(GROUP // 2)], axis=1
             )
-            at_x = (key >> 7) - x0
+            at_x = key >> 7
             at_y = (key & 127).astype(F32)
-            for x in range(half_x):
+            for x in range(nx):
                 kx = jnp.broadcast_to(jnp.where(at_x == x, at_y, -1.0), (16, GROUP * cap)).astype(BF)
                 for q in range(ny // 16):
                     hot = kx == (sub16s + 16.0 * q).astype(BF)
                     ohs[x * ny + q * 16 : x * ny + (q + 1) * 16, :] = jnp.where(
                         hot, jnp.ones((), BF), jnp.zeros((), BF)
                     )
-            rows = recv_rows[j, pl.ds(s0, GROUP)].reshape(GROUP * cap, vals)
+            rows = recv_rows[pl.ds(s0, GROUP)].reshape(GROUP * cap, vals)
             acc[...] += jnp.dot(ohs[...], rows, preferred_element_type=F32)
             return 0
 
@@ -378,16 +381,44 @@
             acc[...] = jnp.zeros_like(acc)
         lax.fori_loop(first, last, unpack, 0)
 
-    def share(j):
-        part = g_s.at[c + 2 * j]
-        return remote(part, part, gs_sem.at[j], gr_sem.at[j], core, t)
-
-    def share_sums(j):
-        total = acc[...]
+    def sums_to_core(k):
+        part = g_s.at[mine, pl.ds(2 * k, 2)]
+        return remote(part, part, gks.at[k], gkr.at[k], core, t)
+
+    def sums_to_far(k):
+        return remote(g_far.at[pl.ds(2 * k, 2)], g_s.at[mine, pl.ds(2 * k, 2)], gzs.at[k], gzr.at[k], far, t)
+
+    def sums_pass_on(k):
+        part = g_s.at[far, pl.ds(2 * k, 2)]
+        return remote(part, part, gfs.at[k], gfr.at[k], core, t)
+
+    def two_parts(x):
+        total = acc[pl.ds(pl.multiple_of(x * ny, ny), ny), :]
         head = total.astype(BF)
-        g_s[c + 2 * j, :, :vals] = head
-        g_s[c + 2 * j, :, vals:] = (total - head.astype(F32)).astype(BF)
-        share(j).start()
+        return jnp.concatenate([head, (total - head.astype(F32)).astype(BF)], axis=1)
+
+    def share_sums():
+        for k in range(2):
+            for i in (2 * k, 2 * k + 1):
+                g_far[i] = two_parts(x1 + order[i])
+            sums_to_far(k).start()
+        for k in range(2):
+            for i in (2 * k, 2 * k + 1):
+                g_s[mine, i] = two_parts(x0 + order[i])
+            sums_to_core(k).start()
+
+    def wait_sums(k, half):
+        @pl.when(h != half)
+        def _():
+            sums_to_far(k).wait_recv()
+            sums_pass_on(k).start()
+
+        if half == 0:
+            sums_to_core(k).wait_recv()
+
+        @pl.when(h != half)
+        def _():
+            sums_pass_on(k).wait_recv()
 
     for i in range(1, half_x - 1):
         swap_lam[i].wait_recv()
@@ -396,37 +427,46 @@
     def _():
         cx_west.wait_recv()
 
-    inner = list(range(1, half_x - 1))
-    outer = [0, half_x - 1]
     for x in inner:
         dyn(0, x, a_s, b_s)
+    read_cells()
+    sum_rows(0, groups)
+    share_sums()
     wait_halos(0)
     for x in outer:
         dyn(0, x, a_s, b_s)
-    read_cells()
-    sum_rows(0, 0, groups)
-    share_sums(0)
     swap_op.wait_recv()
     now, new = b_s, a_s
+    last = a_s if steps % 2 == 0 else b_s
+
+    def keep(x):
+        return pltpu.make_async_copy(last.at[x, h], out_hbm.at[x0 + x], ls.at[x])
+
+    def give(at, x):
+        return remote(last.at[x, 1 - h], out_hbm.at[at + x], ts.at[x], tr.at[x], far, t)
+
+    def finish(xs):
+        for x in xs:
+            give(x0, x).start()
+            keep(x).start()
+
     for n in range(steps):
         if n == 0:
-            share(0).wait_recv()
+            wait_sums(0, 0)
         if n == 2:
-            share(1).wait_recv()
+            wait_sums(0, 1)
+            wait_sums(1, 1)
         phys(n, outer, now)
         if n + 1 < steps:
             send_halos(n + 1, now)
         else:
-            finish(outer, now, fin_in, ts, tr, h, far, t, remote)
+            finish(outer)
+        if n == 0:
+            wait_sums(1, 0)
         phys(n, inner, now)
         if n + 1 == steps:
-            finish(inner, now, fin_in, ts, tr, h, far, t, remote)
+            finish(inner)
             break
-        if n == 0:
-            sum_rows(1, 0, groups // 2)
-        if n == 1:
-            sum_rows(1, groups // 2, groups)
-            share_sums(1)
         for x in inner:
             dyn(n + 1, x, now, new)
         wait_halos(n + 1)
@@ -434,29 +474,25 @@
             dyn(n + 1, x, now, new)
         now, new = new, now
 
-    for i in range(half_x):
-        out_ref[pl.ds(x0 + i, width, stride=nx), :] = now[i, h]
-    for i in outer + inner:
-        remote(now.at[i, 1 - h], fin_in.at[i], ts.at[i], tr.at[i], far, t).wait_recv()
-        out_ref[pl.ds(x1 + i, width, stride=nx), :] = fin_in[i]
-
-    def drain(i, _):
-        d = (t + i) % n_tile
-        cell_copy(d).wait_send()
-        for j in range(2):
-            row_copy(j, d).wait_send()
-        return 0
-
-    lax.fori_loop(1, n_tile, drain, 0)
-    for copy in [swap_misc, swap_op] + swap_lam + [share(0), share(1)]:
+    for x in outer + inner:
+        keep(x).wait()
+        give(x1, x).wait_recv()
+
+    all_of(send_cell.at[0, pl.ds(0, n_tile - 1), :], ss_cell, rs_cell).wait_send()
+    all_of(send_rows.at[pl.ds(0, n_tile - 1)], ss_rows, rs_rows.at[0]).wait_send()
+    for copy in [swap_misc, swap_op] + swap_lam:
         copy.wait_send()
+    for k in range(2):
+        sums_to_core(k).wait_send()
+        sums_to_far(k).wait_send()
+        sums_pass_on(k).wait_send()
 
     @pl.when(cx_goes)
     def _():
         cx_west.wait_send()
 
     for i in range(half_x):
-        remote(now.at[i, 1 - h], fin_in.at[i], ts.at[i], tr.at[i], far, t).wait_send()
+        give(x0, i).wait_send()
     for n in range(steps):
         for x in range(half_x):
             to_core(n, x).wait_send()
@@ -468,11 +504,6 @@
         @pl.when(has_east)
         def _(n=n):
             to_east(n).wait_send()
-
-
-def finish(xs, now, fin_in, ts, tr, h, far, t, remote):
-    for x in xs:
-        remote(now.at[x, 1 - h], fin_in.at[x], ts.at[x], tr.at[x], far, t).start()
 
 
 def place_of(levels_all, lev_here, fields):
@@ -512,24 +543,28 @@
     dma = pltpu.SemaphoreType.DMA
     out = pl.pallas_call(
         kernel,
-        out_shape=jax.ShapeDtypeStruct((width * nx, ny), F32),
-        in_specs=[vmem] * 8 + [pl.BlockSpec(memory_space=pltpu.SMEM)] + [hbm] * 3,
-        out_specs=vmem,
+        out_shape=jax.ShapeDtypeStruct((nx, width, ny), F32),
+        in_specs=[vmem] * 5 + [pl.BlockSpec(memory_space=pltpu.SMEM)] + [hbm] * 6,
+        out_specs=hbm,
         scratch_shapes=[
+            V((width * nx, ny), F32),
+            V((nl * nx, ny), F32),
+            V((nl * nx, ny), F32),
             V((2, obs, vals), BF),
-            V((2, n_tile, cap, vals), BF),
-            V((2, n_tile, cap, vals), BF),
-            V((n_tile, 128), F32),
+            V((n_tile, cap, vals), BF),
+            V((n_tile, cap, vals), BF),
+            V((2, n_tile, 128), F32),
             V((n_tile, 128), F32),
             V((n_tile, obs), BF),
             V((2 * cap, obs), BF),
             V((2, 1, obs), F32),
             V((2, 1, obs), jnp.int32),
             V((GROUP * cap, obs), BF),
-            V((2, n_tile // 2, 128), jnp.int32),
-            V((hx * ny, GROUP * cap), BF),
-            V((hx * ny, vals), F32),
-            V((steps, hx * ny, 2 * vals), BF),
+            V((n_tile // 2, 128), jnp.int32),
+            V((nx * ny, GROUP * cap), BF),
+            V((nx * ny, vals), F32),
+            V((steps, hx, ny, 2 * vals), BF),
+            V((hx, ny, 2 * vals), BF),
             V((hx, 2, width, ny), F32),
             V((hx, 2, width, ny), F32),
             V((hx, width, ny), F32),
@@ -546,30 +581,30 @@
             V((steps, 2, 2 * nl, ny), BF),
             V((2, nl, ny), F32),
             V((2, nl, ny), F32),
-            V((hx, width, ny), F32),
-            dma((4,)), dma((2, n_tile)), dma((2, n_tile)), dma((n_tile,)), dma((n_tile,)), dma((2,)), dma((2,)),
+            dma((7,)), dma, dma((n_tile // GROUP,)), dma, dma,
+            dma((2,)), dma((2,)), dma((2,)), dma((2,)), dma((2,)), dma((2,)),
             dma((hx + 2,)), dma((hx + 2,)), dma((steps,)), dma((steps,)), dma((steps,)), dma((steps,)),
-            dma, dma, dma((steps, hx)), dma((steps, hx)), dma((hx,)), dma((hx,)),
+            dma, dma, dma((steps, hx)), dma((steps, hx)), dma((hx,)), dma((hx,)), dma((hx,)),
         ],
         compiler_params=pltpu.CompilerParams(
             collective_id=0, has_side_effects=True, vmem_limit_bytes=56 * 1024 * 1024
         ),
         name="sweep",
     )(
-        adjoint_final.reshape(width * nx, ny),
-        courant_x.reshape(nl * nx, ny),
-        courant_y.reshape(nl * nx, ny),
         sound.reshape(1, nl),
         regime.reshape(steps * nx, ny),
         obs_operator.transpose(1, 2, 0).reshape(width, vals),
         obs_owner.reshape(steps, 1, obs),
         obs_cell,
         obs_count.reshape(1, steps),
+        adjoint_final.reshape(width * nx, ny),
+        courant_x.reshape(nl * nx, ny),
+        courant_y.reshape(nl * nx, ny),
         phys_jac,
         perm,
         obs_rows,
     )
-    return out.reshape(adjoint_final.shape)
+    return out.reshape(nx, fields, nl, ny).transpose(1, 2, 0, 3)
 
 
 def solution(mesh):

time: 119 us -> 111 us (0.933)
  the two profiles are of different devices: /device:TPU:63 before, /device:TPU:97 now
where the time goes in v1:
time: 111 us
  Pallas kernels  109 us (98%)
  local copies, waits for them, and re-layouts  2.07 us (2%)
    pallas_call x1, Pallas kernels, on_device(): pl.pallas_call(kernel, out_shape=jax.ShapeDtypeStruct((nx, width, ny), F3...  109 us

profile of v1, /device:TPU:97, one launch (start us, length us, event | category | flops | bytes accessed | tf_op | source)
XLA Modules:
  0.0 110.6 jit_solution(16564347372850024791)
XLA Ops:
  0.0 108.6 %sweep.1 = f32[8,144,128]{2,1,0:T(8,128)} custom-call(f32[1,24]{1,0:T(1,128)} %bitcast.21, s32[32,128]{1,0:T(8,128)} %bitcast.20, bf16[144,128]{1,0:T(8,128)(2,1)} %bitcast.18, s32[4,1,2048]{2,1,0:T(1,128)} %bitcast.19, s32[4,2048]{1,0:T(4,128)} %cell_ref.1, s32[1,4]{1,0:T(1,128)} %bitcast.22, f32[1152,128]{1,0:T(8,128)} %bitcast.15, f32[192,128]{1,0:T(8,128)} %bitcast.16, ...), custom_call_target="tpu_custom_call" | custom-call | tf_op jit(solution)/shard_map/sweep/pallas_call | solution.py:544
  108.6 2.1 %copy.15 = f32[8,6,24,128]{3,0,2,1:T(8,128)} copy(f32[8,6,24,128]{3,2,1,0:T(8,128)} %bitcast.14) | data formatting | bytes 1179648 | tf_op jit(solution)/shard_map/reshape | solution.py:607

commit v2 on v1

--- a/solution.py
+++ b/solution.py
@@ -125,20 +125,6 @@
     def _():
         e_in[...] = jnp.zeros_like(e_in)
 
-    pl.semaphore_wait(barrier, n_tile + 1)
-
-    inner = list(range(1, half_x - 1))
-    outer = [0, half_x - 1]
-    order = outer + inner
-    slot = {x: i for i, x in enumerate(order)}
-    swap_misc = remote(misc_out, misc.at[h], xs_sem.at[half_x], xr_sem.at[half_x], far, t)
-    swap_op = remote(op_s.at[h], op_s.at[h], xs_sem.at[half_x + 1], xr_sem.at[half_x + 1], far, t)
-    swap_lam = [remote(lam_out.at[i], a_s.at[i, h], xs_sem.at[i], xr_sem.at[i], far, t) for i in range(half_x)]
-    swap_misc.start()
-    for i in order:
-        swap_lam[i].start()
-    swap_op.start()
-
     upper = jnp.where(iota((128, 256), 0) < iota((128, 256), 1), 1.0, 0.0).astype(BF)
     lane128 = iota((n_tile, 128), 1)
 
@@ -165,6 +151,24 @@
         key = both * 128.0 + pltpu.roll(both, 64, axis=1)
         return jnp.where(lane128 < 64, key, 0.0)
 
+    for j in (0,):
+        keys = rank_rows(j)
+        send_cell[j] = jnp.where(t % 2 == 0, keys, pltpu.roll(keys, 64, axis=1))
+
+    pl.semaphore_wait(barrier, n_tile + 1)
+
+    inner = list(range(1, half_x - 1))
+    outer = [0, half_x - 1]
+    order = outer + inner
+    slot = {x: i for i, x in enumerate(order)}
+    swap_misc = remote(misc_out, misc.at[h], xs_sem.at[half_x], xr_sem.at[half_x], far, t)
+    swap_op = remote(op_s.at[h], op_s.at[h], xs_sem.at[half_x + 1], xr_sem.at[half_x + 1], far, t)
+    swap_lam = [remote(lam_out.at[i], a_s.at[i, h], xs_sem.at[i], xr_sem.at[i], far, t) for i in range(half_x)]
+    swap_misc.start()
+    for i in order:
+        swap_lam[i].start()
+    swap_op.start()
+
     def cell_copy(d):
         return remote(
             send_cell.at[crosses(t, d, n_tile).astype(jnp.int32), pl.ds(d, 1), :], recv_cell.at[pl.ds(t, 1), :],
@@ -187,7 +191,7 @@
             load.wait()
 
         def pack(g, _):
-            d0 = pl.multiple_of(((g + my_group) % groups) * GROUP, GROUP)
+            d0 = pl.multiple_of(((3 * g + my_group) % groups) * GROUP, GROUP)
             j = crosses(t, d0, n_tile).astype(jnp.int32)
             for i in range(GROUP):
                 key = jnp.where(own_s[j] == d0 + i, rank_s[j], -1.0)
@@ -215,7 +219,7 @@
         lax.fori_loop(0, groups, pack, 0)
         recv_rows[t] = send_rows[t]
 
-    for j in range(2):
+    for j in (1,):
         keys = rank_rows(j)
         send_cell[j] = jnp.where(t % 2 == 0, keys, pltpu.roll(keys, 64, axis=1))
 
@@ -349,7 +353,7 @@
 
     def sum_rows(first, last):
         def unpack(g, _):
-            s0 = pl.multiple_of(((groups - g + my_group) % groups) * GROUP, GROUP)
+            s0 = pl.multiple_of(((5 * g + my_group) % groups) * GROUP, GROUP)
 
             from_group = s0 // GROUP
 

time: 111 us -> 107 us (0.964)
  Pallas kernels: 109 us -> 105 us
    pallas_call x1, Pallas kernels: 109 us -> 105 us  [on_device(): pl.pallas_call(kernel, out_shape=jax.ShapeDtypeStruct((nx, width, ny), F3...]
where the time goes in v2:
time: 107 us
  Pallas kernels  105 us (98%)
  local copies, waits for them, and re-layouts  2.07 us (2%)
    pallas_call x1, Pallas kernels, on_device(): pl.pallas_call(kernel, out_shape=jax.ShapeDtypeStruct((nx, width, ny), F3...  105 us

profile of v2, /device:TPU:97, one launch (start us, length us, event | category | flops | bytes accessed | tf_op | source)
XLA Modules:
  0.0 107.1 jit_solution(17964258155106647646)
XLA Ops:
  0.0 105.0 %sweep.1 = f32[8,144,128]{2,1,0:T(8,128)} custom-call(f32[1,24]{1,0:T(1,128)} %bitcast.21, s32[32,128]{1,0:T(8,128)} %bitcast.20, bf16[144,128]{1,0:T(8,128)(2,1)} %bitcast.18, s32[4,1,2048]{2,1,0:T(1,128)} %bitcast.19, s32[4,2048]{1,0:T(4,128)} %cell_ref.1, s32[1,4]{1,0:T(1,128)} %bitcast.22, f32[1152,128]{1,0:T(8,128)} %bitcast.15, f32[192,128]{1,0:T(8,128)} %bitcast.16, ...), custom_call_target="tpu_custom_call" | custom-call | tf_op jit(solution)/shard_map/sweep/pallas_call | solution.py:548
  105.0 2.1 %copy.15 = f32[8,6,24,128]{3,0,2,1:T(8,128)} copy(f32[8,6,24,128]{3,2,1,0:T(8,128)} %bitcast.14) | data formatting | bytes 1179648 | tf_op jit(solution)/shard_map/reshape | solution.py:611
